TPU v7x, 128 devices: a whole 4x4x4 slice. The times are simulated.
128 devices in a mesh: replica: 8 (over x, y_hi), shard: 16 (over z, y_lo, core).
Axes of the slice: x: 4, y: 4 (y_hi: 2, y_lo: 2; y = y_hi * 2 + y_lo), z: 4, core: 2. Of those that a mesh axis runs over, the one named last changes fastest.
Arguments:
- tokens: bfloat16 [65536, 1920], P(('replica', 'shard')), may hold values from -36 to 36
- timesteps: int32 [256], P(('replica', 'shard')), may hold values from 0 to 63
- table: float32 [64, 2, 1920], replicated, may hold values from -3 to 3
- weight_values: bfloat16 [4864, 1920], P('shard'), may hold values from -0.125 to 0.125
- weight_scales: bfloat16 [4864, 15], P('shard'), may hold values from 0.29882812 to 3
- cotangent: bfloat16 [65536, 4864], P(('replica', 'shard')), may hold values from -24 to 24
Outputs:
- hidden: bfloat16 [65536, 4864], P(('replica', 'shard'))
- grad_weight: float32 [4864, 1920], P('shard')
- grad_tokens: bfloat16 [65536, 1920], P(('replica', 'shard'))
All inputs are finite; a program needn't handle non-finite values.
Results may differ from a plain program's by a relative error of at most 0.02.
Values may be sent and summed in bfloat16 or wider, within the bound.
A program may use at most 256 MiB of HBM per device.

v0:
```python
import jax
import jax.numpy as jnp
from jax import lax
from jax.sharding import PartitionSpec as P

root_two_over_pi = 0.7978845608028654
cubic_coef = 0.044715
epsilon = 1e-06


def gelu_slope(preact):
    inner_term = root_two_over_pi * (preact + cubic_coef * preact * preact * preact)
    tangent = jnp.tanh(inner_term)
    gelu_value = 0.5 * preact * (1.0 + tangent)
    derivative = 0.5 * (1.0 + tangent) + 0.5 * preact * (
        1.0 - tangent * tangent
    ) * root_two_over_pi * (1.0 + 3.0 * cubic_coef * preact * preact)
    return (gelu_value, derivative)


def dequantize(weight_values, weight_scales):
    row_count, features = weight_values.shape
    blocks = weight_scales.shape[1]
    expanded = (
        weight_values.astype(jnp.float32).reshape(row_count, blocks, features // blocks)
        * weight_scales.astype(jnp.float32)[:, :, None]
    )
    return expanded.reshape(row_count, features).astype(jnp.bfloat16)


def modulate(tokens, timesteps, table):
    samples = timesteps.shape[0]
    step_count = table.shape[0]
    features = tokens.shape[1]
    onehot = (timesteps[:, None] == jnp.arange(step_count, dtype=jnp.int32)[None, :]).astype(
        jnp.float32
    )
    picked = jnp.dot(
        onehot, table.reshape(step_count, 2 * features), precision=lax.Precision.HIGHEST
    )
    picked = picked.reshape(samples, 2, features)
    grouped = tokens.astype(jnp.float32).reshape(samples, -1, features)
    centre = grouped - jnp.mean(grouped, axis=2, keepdims=True)
    inverse = lax.rsqrt(jnp.mean(centre * centre, axis=2, keepdims=True) + epsilon)
    normed = centre * inverse
    factor = 1.0 + picked[:, 1][:, None, :]
    moved = (normed * factor + picked[:, 0][:, None, :]).reshape(-1, features).astype(jnp.bfloat16)
    return (moved, normed, inverse, factor)


def normalize_back(grad_moved, normed, inverse, factor):
    samples = normed.shape[0]
    features = normed.shape[2]
    scaled_grad = grad_moved.reshape(samples, -1, features) * factor
    mean_grad = jnp.mean(scaled_grad, axis=2, keepdims=True)
    mean_prod = jnp.mean(scaled_grad * normed, axis=2, keepdims=True)
    result = inverse * (scaled_grad - mean_grad - normed * mean_prod)
    return result.reshape(-1, features).astype(jnp.bfloat16)


def per_device(tokens, timesteps, table, weight_values, weight_scales, cotangent):
    moved, normed, inverse, factor = modulate(tokens, timesteps, table)
    upstream = cotangent.astype(jnp.float32)
    gathered_values, gathered_scales = (
        lax.all_gather(weight_values, "shard", axis=0, tiled=True),
        lax.all_gather(weight_scales, "shard", axis=0, tiled=True),
    )
    weight = dequantize(gathered_values, gathered_scales)
    preact = jnp.einsum("td,fd->tf", moved, weight, preferred_element_type=jnp.float32)
    gelu_value, derivative = gelu_slope(preact)
    hidden = gelu_value.astype(jnp.bfloat16)
    grad_pre = (upstream * derivative).astype(jnp.bfloat16)
    grad_moved = jnp.dot(grad_pre, weight, preferred_element_type=jnp.float32)
    product = lax.dot_general(
        grad_pre, moved, (((0,), (0,)), ((), ())), preferred_element_type=jnp.float32
    )
    rounded = lax.optimization_barrier(product.astype(jnp.bfloat16))
    group_part = lax.psum_scatter(
        rounded.astype(jnp.float32).astype(jnp.bfloat16), "shard", scatter_dimension=0, tiled=True
    )
    grad_weight = lax.psum(group_part, "replica").astype(jnp.float32)
    grad_tokens = normalize_back(grad_moved, normed, inverse, factor)
    return (hidden, grad_weight, grad_tokens)


def solution(mesh):
    placed = (
        P(("replica", "shard"), None),
        P(("replica", "shard")),
        P(),
        P("shard", None),
        P("shard", None),
        P(("replica", "shard"), None),
    )
    return jax.shard_map(
        per_device,
        mesh=mesh,
        in_specs=placed,
        out_specs=(P(("replica", "shard"), None), P("shard", None), P(("replica", "shard"), None)),
        check_vma=False,
    )
```

profile of v0, /device:TPU:0, one launch (start us, length us, event | category | flops | bytes accessed | tf_op | source)
XLA Modules:
  0.0 496.3 jit_solution(2334483835488481920)
XLA Ops:
  7.2 0.0 all-gather.3.cloned.1.call-start
  7.2 0.7 all-gather.3.cloned.1.call-update
  7.9 0.0 reduce-scatter.2.cloned.1.call-start
  8.0 22.6 %all-gather = bf16[16,304,15]{1,2,0:T(8,128)(2,1)S(1)} all-gather(bf16[1,304,15]{1,2,0:T(8,128)(2,1)} %bitcast.51), channel_id=1, replica_groups=mesh['replica'=8,'shard'=16] {'shard'}, dimensions={0}, use_global_device_ids=true | all-gather | bytes 155040 | tf_op jit(solution)/shard_map/all_gather | solution.py:66
  30.7 0.2 reshape.71
  30.9 0.3 convert_reduce_fusion
  31.3 0.7 multiply_reduce_fusion.1
  31.9 0.2 copy-done.2
  32.1 0.4 fusion.11
  32.6 2.5 fusion.10
  35.1 77.8 %all-gather.3.cloned.1.call-done = bf16[4864,1920]{1,0:T(8,128)(2,1)} async-done(((bf16[304,1920]{1,0:T(8,128)(2,1)}), bf16[4864,1920]{1,0:T(8,128)(2,1)}) %all-gather.3.cloned.1.call-update) | async-done | bytes 18677776 | tf_op jit(solution)/shard_map/all_gather | solution.py:65
  112.8 23.3 %copy.18 = bf16[4864,1920]{0,1:T(8,128)(2,1)} copy(bf16[4864,1920]{1,0:T(8,128)(2,1)} %all-gather.3.cloned.1.call-done) | data formatting | bytes 37355520 | tf_op jit(solution)/shard_map/all_gather | solution.py:65
  136.2 17.3 %fusion = bf16[4864,1920]{0,1:T(8,128)(2,1)} fusion(bf16[4864,1920]{0,1:T(8,128)(2,1)} %copy.18, f32[4864,15]{0,1:T(8,128)S(1)} %reshape.71), kind=kLoop, calls=%fused_computation.1 | loop fusion | flops 28016640 | bytes 37647360 | tf_op jit(solution)/shard_map/convert_element_type | solution.py:28
  153.5 21.5 %fusion.9 = (bf16[512,4864]{1,0:T(8,128)(2,1)S(1)}, bf16[512,4864]{1,0:T(8,128)(2,1)}) fusion(bf16[512,4864]{1,0:T(8,128)(2,1)} %param.11, bf16[512,1920]{1,0:T(8,128)(2,1)S(1)} %copy-done.1, bf16[4864,1920]{0,1:T(8,128)(2,1)} %fusion), kind=kOutput, calls=%fused_computation.13 | convolution fusion | flops 9617801216 | bytes 35586048 | tf_op jit(solution)/shard_map/td,fd->tf/dot_general | solution.py:69
  175.0 2.2 copy-done.4
  177.3 15.2 %convolution_convert_fusion = bf16[4864,1920]{1,0:T(8,128)(2,1)} fusion(bf16[512,4864]{1,0:T(8,128)(2,1)S(1)} %get-tuple-element.5, bf16[512,1920]{1,0:T(8,128)(2,1)S(1)} %copy-done.1), kind=kOutput, calls=%fused_computation.2 | convolution fusion | flops 9572352000 | bytes 25624576 | tf_op jit(solution)/shard_map/dot_general | solution.py:74
  192.5 0.0 reduce-scatter.2.cloned.1.call-update
  192.5 0.0 all-reduce.2.cloned.1.call-start
  192.6 203.4 %reduce-scatter.2.cloned.1.call-done = bf16[304,1920]{1,0:T(8,128)(2,1)} async-done(((bf16[4864,1920]{1,0:T(8,128)(2,1)}), bf16[304,1920]{1,0:T(8,128)(2,1)}) %reduce-scatter.2.cloned.1.call-update) | async-done | bytes 1167376 | tf_op jit(solution)/shard_map/reduce_scatter | solution.py:78
  396.0 0.0 all-reduce.2.cloned.1.call-update
  396.0 17.9 %multiply_reduce_fusion.2 = (f32[2,256]{1,0:T(2,128)S(1)}, f32[2,256]{1,0:T(2,128)S(1)}, f32[2,256,1920]{2,1,0:T(8,128)}) fusion(f32[2,1920]{1,0:T(2,128)S(1)} %get-tuple-element.7, f32[2,256]{1,0:T(2,128)S(1)} %rsqrt.13, f32[2,256]{1,0:T(2,128)S(1)} %div.17, bf16[2,256,4864]{2,1,0:T(8,128)(2,1)} %bitcast.52, bf16[4864,1920]{0,1:T(8,128)(2,1)} %fusion, ...), kind=kOutput, calls=%fused_computation.22 | convolution fusion | flops 9569894400 | bytes 29580288 | tf_op jit(solution)/shard_map/dot_general | solution.py:73
  413.9 3.9 multiply_convert_fusion.1
  417.7 69.2 %all-reduce.2.cloned.1.call-done = bf16[304,1920]{1,0:T(8,128)(2,1)} async-done(((bf16[304,1920]{1,0:T(8,128)(2,1)}), bf16[304,1920]{1,0:T(8,128)(2,1)}) %all-reduce.2.cloned.1.call-update) | async-done | bytes 1167376 | tf_op jit(solution)/shard_map/psum | solution.py:81
  487.0 2.8 convert_element_type.48
  (15 shorter events, 0.1 us)
Async XLA Ops:
  7.2 23.7 %copy-start = (bf16[512,1920]{1,0:T(8,128)(2,1)S(1)}, bf16[512,1920]{1,0:T(8,128)(2,1)}, u32[]{:S(2)}) copy-start(bf16[512,1920]{1,0:T(8,128)(2,1)} %param.6) | copy-start | bytes 5898244
  7.2 24.8 %copy-start.3 = (s32[2]{0:T(128)S(1)}, s32[2]{0:T(128)}, u32[]{:S(2)}) copy-start(s32[2]{0:T(128)} %param.7) | copy-start | bytes 28
  7.2 105.7 %all-gather.3.cloned.1.call-start = ((), (), s32[]{:S(2)}) async-start(), calls=%async_computation.1 | async-start | bytes 19845120 | tf_op jit(solution)/shard_map/all_gather | solution.py:65
  7.9 388.0 %reduce-scatter.2.cloned.1.call-start = ((), (), s32[]{:S(2)}) async-start(), calls=%async_computation.2 | async-start | bytes 19845120 | tf_op jit(solution)/shard_map/reduce_scatter | solution.py:78
  30.9 1.2 copy-start.2
  136.2 17.3 %copy-start.1 = (bf16[512,1920]{1,0:T(8,128)(2,1)S(1)}, bf16[512,1920]{1,0:T(8,128)(2,1)}, u32[]{:S(2)}) copy-start(bf16[512,1920]{1,0:T(8,128)(2,1)} %fusion.10) | copy-start | bytes 5898244
  175.0 2.2 copy-start.4
  192.5 294.4 %all-reduce.2.cloned.1.call-start = ((), (), s32[]{:S(2)}) async-start(), calls=%async_computation.3 | async-start | bytes 2334720 | tf_op jit(solution)/shard_map/psum | solution.py:81
Sparse Core Ops, SparseCore 0:
  9.7 103.0 all-gather.2
  192.6 203.2 reduce-scatter.1
  398.6 88.2 all-reduce.1
where the time goes:
time: 497 us; the launch traced here: 496 us
  waiting for transfers between devices  351 us (71%)
  matrix products  55.1 us (11%)
  other arithmetic  27.5 us (6%)
  local copies, waits for them, and re-layouts  26 us (5%)
  blocking collectives  22.6 us (5%)
  between operations  13.8 us (3%)
    reduce_scatter x1, waiting for transfers between devices, per_device(): lax.psum_scatter(rounded.astype(jnp.float32).astype(jnp.bfloat16), 'shard...  203 us
    all_gather x1, waiting for transfers between devices, per_device(): lax.all_gather(weight_values, 'shard', axis=0, tiled=True)  77.8 us
    psum x1, waiting for transfers between devices, per_device(): grad_weight = lax.psum(group_part, 'replica').astype(jnp.float32)  69.2 us
    all_gather x1, local copies, waits for them, and re-layouts, per_device(): lax.all_gather(weight_values, 'shard', axis=0, tiled=True)  23.3 us
    all_gather x1, blocking collectives, per_device(): lax.all_gather(weight_scales, 'shard', axis=0, tiled=True)  22.6 us
    dot_general x1, matrix products, per_device(): jnp.einsum('td,fd->tf', moved, weight, preferred_element_type=jnp.float32)  21.5 us
    dot_general x1, matrix products, per_device(): grad_moved = jnp.dot(grad_pre, weight, preferred_element_type=jnp.float32)  17.9 us
    convert_element_type x1, other arithmetic, dequantize(): return expanded.reshape(row_count, features).astype(jnp.bfloat16)  17.3 us
  transfers between devices with their start and end apart: 3, of which 3 were waited for; matrix products, arithmetic and copies ran while one was open for 5% of the time, Pallas kernels for 0%

commit v1 on v0

--- a/solution.py
+++ b/solution.py
@@ -78,7 +78,7 @@
     group_part = lax.psum_scatter(
         rounded.astype(jnp.float32).astype(jnp.bfloat16), "shard", scatter_dimension=0, tiled=True
     )
-    grad_weight = lax.psum(group_part, "replica").astype(jnp.float32)
+    grad_weight = jnp.sum(lax.all_gather(group_part, "replica"), axis=0).astype(jnp.float32)
     grad_tokens = normalize_back(grad_moved, normed, inverse, factor)
     return (hidden, grad_weight, grad_tokens)
 

time: 497 us -> 530 us (1.066)
  waiting for transfers between devices: 351 us -> 379 us
    all_gather x0 -> x1, waiting for transfers between devices: none -> 97 us  [per_device(): lax.all_gather(group_part, 'replica')]
    psum x1 -> x0, waiting for transfers between devices: 69.2 us -> none  [per_device(): grad_weight = lax.psum(group_part, 'replica').astype(jnp.float32)]
    reduce_sum x0 -> x1, other arithmetic: none -> 5.53 us  [per_device(): jnp.sum(lax.all_gather(group_part, 'replica'), axis=0).astype(jnp.float32)]
where the time goes in v1:
time: 530 us; the launch traced here: 528 us
  waiting for transfers between devices  379 us (72%)
  matrix products  55.1 us (10%)
  other arithmetic  31.8 us (6%)
  local copies, waits for them, and re-layouts  26 us (5%)
  blocking collectives  22.6 us (4%)
  between operations  13.8 us (3%)
    reduce_scatter x1, waiting for transfers between devices, per_device(): lax.psum_scatter(rounded.astype(jnp.float32).astype(jnp.bfloat16), 'shard...  203 us
    all_gather x1, waiting for transfers between devices, per_device(): lax.all_gather(group_part, 'replica')  97 us
    all_gather x1, waiting for transfers between devices, per_device(): lax.all_gather(weight_values, 'shard', axis=0, tiled=True)  77.8 us
    all_gather x1, local copies, waits for them, and re-layouts, per_device(): lax.all_gather(weight_values, 'shard', axis=0, tiled=True)  23.3 us
    all_gather x1, blocking collectives, per_device(): lax.all_gather(weight_scales, 'shard', axis=0, tiled=True)  22.6 us
    dot_general x1, matrix products, per_device(): jnp.einsum('td,fd->tf', moved, weight, preferred_element_type=jnp.float32)  21.5 us
    dot_general x1, matrix products, per_device(): grad_moved = jnp.dot(grad_pre, weight, preferred_element_type=jnp.float32)  17.9 us
    convert_element_type x1, other arithmetic, dequantize(): return expanded.reshape(row_count, features).astype(jnp.bfloat16)  17.3 us
  transfers between devices with their start and end apart: 3, of which 3 were waited for; matrix products, arithmetic and copies ran while one was open for 5% of the time, Pallas kernels for 0%

profile of v1, /device:TPU:0, one launch (start us, length us, event | category | flops | bytes accessed | tf_op | source)
XLA Modules:
  0.0 528.4 jit_solution(6311239397062002841)
XLA Ops:
  7.2 0.0 all-gather.5.cloned.1.call-start
  7.2 0.7 all-gather.5.cloned.1.call-update
  7.9 0.0 reduce-scatter.2.cloned.1.call-start
  8.0 22.6 %all-gather.1 = bf16[16,304,15]{1,2,0:T(8,128)(2,1)S(1)} all-gather(bf16[1,304,15]{1,2,0:T(8,128)(2,1)} %bitcast.53), channel_id=1, replica_groups=mesh['replica'=8,'shard'=16] {'shard'}, dimensions={0}, use_global_device_ids=true | all-gather | bytes 155040 | tf_op jit(solution)/shard_map/all_gather | solution.py:66
  30.7 0.2 reshape.72
  30.9 0.3 convert_reduce_fusion
  31.3 0.7 multiply_reduce_fusion.1
  31.9 0.2 copy-done.2
  32.1 0.4 fusion.11
  32.6 2.5 fusion.10
  35.1 77.8 %all-gather.5.cloned.1.call-done = bf16[4864,1920]{1,0:T(8,128)(2,1)} async-done(((bf16[304,1920]{1,0:T(8,128)(2,1)}), bf16[4864,1920]{1,0:T(8,128)(2,1)}) %all-gather.5.cloned.1.call-update) | async-done | bytes 18677776 | tf_op jit(solution)/shard_map/all_gather | solution.py:65
  112.8 23.3 %copy.18 = bf16[4864,1920]{0,1:T(8,128)(2,1)} copy(bf16[4864,1920]{1,0:T(8,128)(2,1)} %all-gather.5.cloned.1.call-done) | data formatting | bytes 37355520 | tf_op jit(solution)/shard_map/all_gather | solution.py:65
  136.2 17.3 %fusion = bf16[4864,1920]{0,1:T(8,128)(2,1)} fusion(bf16[4864,1920]{0,1:T(8,128)(2,1)} %copy.18, f32[4864,15]{0,1:T(8,128)S(1)} %reshape.72), kind=kLoop, calls=%fused_computation.1 | loop fusion | flops 28016640 | bytes 37647360 | tf_op jit(solution)/shard_map/convert_element_type | solution.py:28
  153.5 21.5 %fusion.9 = (bf16[512,4864]{1,0:T(8,128)(2,1)S(1)}, bf16[512,4864]{1,0:T(8,128)(2,1)}) fusion(bf16[512,4864]{1,0:T(8,128)(2,1)} %param.11, bf16[512,1920]{1,0:T(8,128)(2,1)S(1)} %copy-done.1, bf16[4864,1920]{0,1:T(8,128)(2,1)} %fusion), kind=kOutput, calls=%fused_computation.13 | convolution fusion | flops 9617801216 | bytes 35586048 | tf_op jit(solution)/shard_map/td,fd->tf/dot_general | solution.py:69
  175.0 2.2 copy-done.4
  177.3 15.2 %convolution_convert_fusion = bf16[4864,1920]{1,0:T(8,128)(2,1)} fusion(bf16[512,4864]{1,0:T(8,128)(2,1)S(1)} %get-tuple-element.5, bf16[512,1920]{1,0:T(8,128)(2,1)S(1)} %copy-done.1), kind=kOutput, calls=%fused_computation.2 | convolution fusion | flops 9572352000 | bytes 25624576 | tf_op jit(solution)/shard_map/dot_general | solution.py:74
  192.5 0.0 reduce-scatter.2.cloned.1.call-update
  192.5 0.0 all-gather.7.cloned.1.call-start
  192.6 203.4 %reduce-scatter.2.cloned.1.call-done = bf16[304,1920]{1,0:T(8,128)(2,1)} async-done(((bf16[4864,1920]{1,0:T(8,128)(2,1)}), bf16[304,1920]{1,0:T(8,128)(2,1)}) %reduce-scatter.2.cloned.1.call-update) | async-done | bytes 1167376 | tf_op jit(solution)/shard_map/reduce_scatter | solution.py:78
  396.0 17.9 %multiply_reduce_fusion.2 = (f32[2,256]{1,0:T(2,128)S(1)}, f32[2,256]{1,0:T(2,128)S(1)}, f32[2,256,1920]{2,1,0:T(8,128)}) fusion(f32[2,1920]{1,0:T(2,128)S(1)} %get-tuple-element.7, f32[2,256]{1,0:T(2,128)S(1)} %rsqrt.13, f32[2,256]{1,0:T(2,128)S(1)} %div.17, bf16[2,256,4864]{2,1,0:T(8,128)(2,1)} %bitcast.54, bf16[4864,1920]{0,1:T(8,128)(2,1)} %fusion, ...), kind=kOutput, calls=%fused_computation.22 | convolution fusion | flops 9569894400 | bytes 29580288 | tf_op jit(solution)/shard_map/dot_general | solution.py:73
  413.9 3.9 multiply_convert_fusion.1
  417.8 97.0 %all-gather.7.cloned.1.call-done = bf16[2432,1920]{1,0:T(8,128)(2,1)} async-done(((bf16[304,1920]{1,0:T(8,128)(2,1)}), bf16[2432,1920]{1,0:T(8,128)(2,1)}) %all-gather.7.cloned.1.call-update) | async-done | bytes 9338896 | tf_op jit(solution)/shard_map/all_gather | solution.py:81
  514.8 5.5 %reduce_sum.50 = bf16[304,1920]{1,0:T(8,128)(2,1)S(1)} reduce(bf16[8,304,1920]{2,1,0:T(8,128)(2,1)} %bitcast.50, bf16[]{:T(256)} %constant.22.clone.1), dimensions={0}, to_apply=%region_3.0 | reduce | flops 4085760 | bytes 10506242 | tf_op jit(solution)/shard_map/reduce_sum | solution.py:81
  520.3 1.5 convert_element_type.50
  (16 shorter events, 0.1 us)
Async XLA Ops:
  7.2 23.7 %copy-start = (bf16[512,1920]{1,0:T(8,128)(2,1)S(1)}, bf16[512,1920]{1,0:T(8,128)(2,1)}, u32[]{:S(2)}) copy-start(bf16[512,1920]{1,0:T(8,128)(2,1)} %param.6) | copy-start | bytes 5898244
  7.2 24.8 %copy-start.3 = (s32[2]{0:T(128)S(1)}, s32[2]{0:T(128)}, u32[]{:S(2)}) copy-start(s32[2]{0:T(128)} %param.7) | copy-start | bytes 28
  7.2 105.7 %all-gather.5.cloned.1.call-start = ((), (), s32[]{:S(2)}) async-start(), calls=%async_computation.1 | async-start | bytes 19845120 | tf_op jit(solution)/shard_map/all_gather | solution.py:65
  7.9 388.0 %reduce-scatter.2.cloned.1.call-start = ((), (), s32[]{:S(2)}) async-start(), calls=%async_computation.2 | async-start | bytes 19845120 | tf_op jit(solution)/shard_map/reduce_scatter | solution.py:78
  30.9 1.2 copy-start.2
  136.2 17.3 %copy-start.1 = (bf16[512,1920]{1,0:T(8,128)(2,1)S(1)}, bf16[512,1920]{1,0:T(8,128)(2,1)}, u32[]{:S(2)}) copy-start(bf16[512,1920]{1,0:T(8,128)(2,1)} %fusion.10) | copy-start | bytes 5898244
  175.0 2.2 copy-start.4
  192.5 322.3 %all-gather.7.cloned.1.call-start = ((), (), s32[]{:S(2)}) async-start(), calls=%async_computation.3 | async-start | bytes 10506240 | tf_op jit(solution)/shard_map/all_gather | solution.py:81
Sparse Core Ops, SparseCore 0:
  9.7 103.0 all-gather.4
  192.6 203.2 reduce-scatter.1
  398.6 116.1 all-gather.6
